TPU v7x, 512 devices: a whole 4x8x8 slice. The times are simulated.
512 devices in a mesh: group: 64 (over x, z, core), head: 8 (over y).
Axes of the slice: x: 4, y: 8, z: 8, core: 2. Of those that a mesh axis runs over, the one named last changes fastest.
Arguments:
- tokens: bfloat16 [16384, 3072], P(('group', 'head')), may hold values from -10 to 10
- attn_gain: float32 [3072], replicated, may hold values from 0.25 to 1.75
- w_query: bfloat16 [3072, 1536], P('group', 'head'), may hold values from -1 to 1
- w_key: bfloat16 [3072, 1536], P('group', 'head'), may hold values from -1 to 1
- w_value: bfloat16 [3072, 1536], P('group', 'head'), may hold values from -0.109375 to 0.109375
- w_out: bfloat16 [1536, 3072], P('head', 'group'), may hold values from -0.15625 to 0.15625
- mlp_gain: float32 [3072], replicated, may hold values from 0.25 to 1.75
- w_gate: bfloat16 [3072, 4096], P('group', 'head'), may hold values from -0.109375 to 0.109375
- w_up: bfloat16 [3072, 4096], P('group', 'head'), may hold values from -0.109375 to 0.109375
- w_down: bfloat16 [4096, 3072], P('head', 'group'), may hold values from -0.09375 to 0.09375
- segment_ids: int32 [64, 256], P('group'), may hold values from 0 to 3, never falling along the last dimension, each value on 1 to 128 neighbouring positions
- cache_slot: int32 [64, 256], P('group'), may hold values from 0 to 255, each once within a row
Outputs:
- layer_out: bfloat16 [16384, 3072], P(('group', 'head'))
- cache_keys: bfloat16 [16384, 1536], P('group', 'head')
- cache_values: bfloat16 [16384, 1536], P('group', 'head')
Inputs may be any that keep to these rules, and one draw needn't show every extreme that they name: `segment_ids`: within each group, segment ids never fall; each of the 4 prompts has 1 to 128 tokens and one has exactly 128. `cache_slot`: each group's row of cache slots holds every slot once.
All inputs are finite; a program needn't handle non-finite values.
Results may differ from a plain program's by a relative error of at most 0.018.
Values may be sent and summed in bfloat16 or wider, within the bound.
A program may use at most 64 MiB of HBM per device.

v0:
```python
import jax
import jax.numpy as jnp
from jax import lax
from jax.sharding import PartitionSpec as P

HEAD_DIM = 96


def norm_rows(rows, gain):
    values = rows.astype(jnp.float32)
    scale = lax.rsqrt(jnp.mean(values * values, axis=-1, keepdims=True) + 1e-05)
    return (values * scale * gain).astype(jnp.bfloat16)


def positions(segment):
    count = segment.shape[0]
    index = jnp.arange(count, dtype=jnp.int32)
    before = jnp.concatenate([jnp.full((1,), -1, jnp.int32), segment[:-1]])
    starts = jnp.where(segment != before, index, jnp.zeros_like(index))
    return index - lax.cummax(starts, axis=0)


def rotate(heads, place):
    half = heads.shape[-1] // 2
    freq = 10000.0 ** (-2.0 * jnp.arange(half, dtype=jnp.float32) / heads.shape[-1])
    angle = place.astype(jnp.float32)[:, None] * freq[None, :]
    cosine = jnp.cos(angle)[:, None, :]
    sine = jnp.sin(angle)[:, None, :]
    first = heads[..., :half]
    second = heads[..., half:]
    return jnp.concatenate(
        [first * cosine - second * sine, second * cosine + first * sine], axis=-1
    )


def accumulate(source, pieces):
    return tuple((jnp.dot(source, piece, preferred_element_type=jnp.float32) for piece in pieces))


def per_device(
    tokens,
    attn_gain,
    w_query,
    w_key,
    w_value,
    w_out,
    mlp_gain,
    w_gate,
    w_up,
    w_down,
    segment_ids,
    cache_slot,
):
    width = w_query.shape[1]
    heads_here = width // HEAD_DIM
    normed = norm_rows(tokens, attn_gain)
    whole = lax.all_gather(normed, "head", axis=0, tiled=True)
    count = whole.shape[0]
    query, key, value = accumulate(
        whole,
        (
            lax.all_gather(w_query, "group", axis=0, tiled=True),
            lax.all_gather(w_key, "group", axis=0, tiled=True),
            lax.all_gather(w_value, "group", axis=0, tiled=True),
        ),
    )
    segment = segment_ids[0]
    place = positions(segment)
    q_rot = rotate(query.reshape(count, heads_here, HEAD_DIM), place).astype(jnp.bfloat16)
    k_rot = rotate(key.reshape(count, heads_here, HEAD_DIM), place).astype(jnp.bfloat16)
    v_b = value.astype(jnp.bfloat16)
    slots = cache_slot[0]
    k_flat = k_rot.reshape(count, width)
    cache_keys = jnp.zeros_like(k_flat).at[slots].set(k_flat)
    cache_values = jnp.zeros_like(v_b).at[slots].set(v_b)
    index = jnp.arange(count, dtype=jnp.int32)
    allowed = (segment[:, None] == segment[None, :]) & (index[None, :] <= index[:, None])
    scores = jnp.einsum("qhd,khd->hqk", q_rot, k_rot, preferred_element_type=jnp.float32)
    scores = scores * (1.0 / HEAD_DIM**0.5)
    scores = jnp.where(allowed[None, :, :], scores, -1e30)
    top = jnp.max(scores, axis=-1, keepdims=True)
    expo = jnp.exp(scores - top)
    probs = (expo / jnp.sum(expo, axis=-1, keepdims=True)).astype(jnp.bfloat16)
    v_heads = v_b.reshape(count, heads_here, HEAD_DIM)
    attended = jnp.einsum("hqk,khd->qhd", probs, v_heads, preferred_element_type=jnp.float32)
    attended = attended.astype(jnp.bfloat16).reshape(count, width)
    out_terms = jnp.dot(
        attended,
        lax.all_gather(w_out, "group", axis=1, tiled=True),
        preferred_element_type=jnp.float32,
    )
    attn_rows = lax.psum_scatter(
        out_terms.astype(jnp.bfloat16), "head", scatter_dimension=0, tiled=True
    ).astype(jnp.float32)
    middle = (tokens.astype(jnp.float32) + attn_rows).astype(jnp.bfloat16)
    normed2 = norm_rows(middle, mlp_gain)
    mlp_in = lax.all_gather(normed2, "head", axis=0, tiled=True)
    gate, up = accumulate(
        mlp_in,
        (
            lax.all_gather(w_gate, "group", axis=0, tiled=True),
            lax.all_gather(w_up, "group", axis=0, tiled=True),
        ),
    )
    hidden = (jax.nn.silu(gate) * up).astype(jnp.bfloat16)
    down_terms = jnp.dot(
        hidden,
        lax.all_gather(w_down, "group", axis=1, tiled=True),
        preferred_element_type=jnp.float32,
    )
    mlp_rows = lax.psum_scatter(
        down_terms.astype(jnp.bfloat16), "head", scatter_dimension=0, tiled=True
    ).astype(jnp.float32)
    layer_out = (middle.astype(jnp.float32) + mlp_rows).astype(jnp.bfloat16)
    return (layer_out, cache_keys, cache_values)


def solution(mesh):
    in_specs = (
        P(("group", "head"), None),
        P(),
        P("group", "head"),
        P("group", "head"),
        P("group", "head"),
        P("head", "group"),
        P(),
        P("group", "head"),
        P("group", "head"),
        P("head", "group"),
        P("group", None),
        P("group", None),
    )
    out_specs = (P(("group", "head"), None), P("group", "head"), P("group", "head"))
    return jax.shard_map(
        per_device, mesh=mesh, in_specs=in_specs, out_specs=out_specs, check_vma=False
    )
```

profile of v0, /device:TPU:6, one launch (start us, length us, event | category | flops | bytes accessed | tf_op | source)
XLA Modules:
  0.0 791.9 jit_solution(14705716523494521434)
XLA Ops:
  7.2 0.7 all-gather.16.cloned.1.call-update
  7.9 1.1 fusion.10
  9.0 1.7 fusion.12
  10.8 0.7 all-gather.14.cloned.1.call-update
  12.7 0.8 compare_select_fusion.1
  14.5 0.9 fusion.19
  15.3 82.9 %all-gather.16.cloned.1.call-done = bf16[3072,192]{1,0:T(8,128)(2,1)} async-done(((bf16[48,192]{1,0:T(8,128)(2,1)}), bf16[3072,192]{1,0:T(8,128)(2,1)}) %all-gather.16.cloned.1.call-update) | async-done | bytes 1179664 | tf_op jit(solution)/shard_map/all_gather | solution.py:63
  98.2 43.3 %all-gather.10.cloned.1.call-done = bf16[256,3072]{1,0:T(8,128)(2,1)} async-done(((bf16[32,3072]{1,0:T(8,128)(2,1)}), bf16[256,3072]{1,0:T(8,128)(2,1)}) %all-gather.10.cloned.1.call-update) | async-done | bytes 1572880 | tf_op jit(solution)/shard_map/all_gather | solution.py:57
  141.5 2.8 fusion.41
  144.3 81.7 %all-gather.14.cloned.1.call-done = bf16[3072,192]{1,0:T(8,128)(2,1)} async-done(((bf16[48,192]{1,0:T(8,128)(2,1)}), bf16[3072,192]{1,0:T(8,128)(2,1)}) %all-gather.14.cloned.1.call-update) | async-done | bytes 1179664 | tf_op jit(solution)/shard_map/all_gather | solution.py:62
  226.0 2.2 fusion.40
  228.9 80.6 %all-gather.12.cloned.1.call-done = bf16[3072,192]{1,0:T(8,128)(2,1)} async-done(((bf16[48,192]{1,0:T(8,128)(2,1)}), bf16[3072,192]{1,0:T(8,128)(2,1)}) %all-gather.12.cloned.1.call-update) | async-done | bytes 1179664 | tf_op jit(solution)/shard_map/all_gather | solution.py:64
  309.5 2.2 convolution_convert_fusion.2
  312.0 81.1 %all-gather.18.cloned.1.call-done = bf16[192,3072]{0,1:T(8,128)(2,1)} async-done(((bf16[192,48]{0,1:T(8,128)(2,1)}), bf16[192,3072]{0,1:T(8,128)(2,1)}) %all-gather.18.cloned.1.call-update) | async-done | bytes 1179664 | tf_op jit(solution)/shard_map/all_gather | solution.py:89
  393.1 3.2 convolution_convert_fusion.1
  396.3 0.7 all-gather.22.cloned.1.call-update
  397.1 40.2 %reduce-scatter.3.cloned.1.call-done = bf16[32,3072]{1,0:T(8,128)(2,1)} async-done(((bf16[256,3072]{1,0:T(8,128)(2,1)}), bf16[32,3072]{1,0:T(8,128)(2,1)}) %reduce-scatter.3.cloned.1.call-update) | async-done | bytes 196624 | tf_op jit(solution)/shard_map/reduce_scatter | solution.py:92
  437.2 1.1 fusion.14
  438.4 1.7 fusion.16
  440.2 0.7 all-gather.24.cloned.1.call-update
  441.5 81.5 %all-gather.22.cloned.1.call-done = bf16[3072,512]{1,0:T(8,128)(2,1)} async-done(((bf16[48,512]{1,0:T(8,128)(2,1)}), bf16[3072,512]{1,0:T(8,128)(2,1)}) %all-gather.22.cloned.1.call-update) | async-done | bytes 3145744 | tf_op jit(solution)/shard_map/all_gather | solution.py:101
  523.0 43.2 %all-gather.20.cloned.1.call-done = bf16[256,3072]{1,0:T(8,128)(2,1)} async-done(((bf16[32,3072]{1,0:T(8,128)(2,1)}), bf16[256,3072]{1,0:T(8,128)(2,1)}) %all-gather.20.cloned.1.call-update) | async-done | bytes 1572880 | tf_op jit(solution)/shard_map/all_gather | solution.py:97
  566.2 3.3 fusion.42
  569.5 82.3 %all-gather.24.cloned.1.call-done = bf16[3072,512]{1,0:T(8,128)(2,1)} async-done(((bf16[48,512]{1,0:T(8,128)(2,1)}), bf16[3072,512]{1,0:T(8,128)(2,1)}) %all-gather.24.cloned.1.call-update) | async-done | bytes 3145744 | tf_op jit(solution)/shard_map/all_gather | solution.py:102
  651.8 84.6 %all-gather.26.cloned.1.call-done = bf16[512,3072]{0,1:T(8,128)(2,1)} async-done(((bf16[512,48]{0,1:T(8,128)(2,1)}), bf16[512,3072]{0,1:T(8,128)(2,1)}) %all-gather.26.cloned.1.call-update) | async-done | bytes 3145744 | tf_op jit(solution)/shard_map/all_gather | solution.py:108
  736.4 6.3 convolution_convert_fusion
  743.6 1.5 scatter_custom_fusion
  745.1 0.7 copy.19
  745.9 1.5 scatter_custom_fusion.1
  747.4 0.7 copy.20
  748.1 35.5 %reduce-scatter.5.cloned.1.call-done = bf16[32,3072]{1,0:T(8,128)(2,1)} async-done(((bf16[256,3072]{1,0:T(8,128)(2,1)}), bf16[32,3072]{1,0:T(8,128)(2,1)}) %reduce-scatter.5.cloned.1.call-update) | async-done | bytes 196624 | tf_op jit(solution)/shard_map/reduce_scatter | solution.py:111
  783.7 1.7 fusion.17
  (46 shorter events, 4.9 us)
Async XLA Ops:
  7.2 91.0 %all-gather.16.cloned.1.call-start = ((), (), s32[]{:S(2)}) async-start(), calls=%async_computation.5 | async-start | bytes 1597440 | tf_op jit(solution)/shard_map/all_gather | solution.py:63
  7.9 133.6 %all-gather.10.cloned.1.call-start = ((), (), s32[]{:S(2)}) async-start(), calls=%async_computation.2 | async-start | bytes 1769472 | tf_op jit(solution)/shard_map/all_gather | solution.py:57
  10.8 215.2 %all-gather.14.cloned.1.call-start = ((), (), s32[]{:S(2)}) async-start(), calls=%async_computation.4 | async-start | bytes 1597440 | tf_op jit(solution)/shard_map/all_gather | solution.py:62
  11.5 298.0 %all-gather.12.cloned.1.call-start = ((), (), s32[]{:S(2)}) async-start(), calls=%async_computation.3 | async-start | bytes 1597440 | tf_op jit(solution)/shard_map/all_gather | solution.py:64
  12.1 381.0 %all-gather.18.cloned.1.call-start = ((), (), s32[]{:S(2)}) async-start(), calls=%async_computation.6 | async-start | bytes 1597440 | tf_op jit(solution)/shard_map/all_gather | solution.py:89
  12.7 424.6 %reduce-scatter.3.cloned.1.call-start = ((), (), s32[]{:S(2)}) async-start(), calls=%async_computation.7 | async-start | bytes 1769472 | tf_op jit(solution)/shard_map/reduce_scatter | solution.py:92
  141.5 84.5 %copy-start = (bf16[256,3072]{1,0:T(8,128)(2,1)S(1)}, bf16[256,3072]{1,0:T(8,128)(2,1)}, u32[]{:S(2)}) copy-start(bf16[256,3072]{1,0:T(8,128)(2,1)} %all-gather.10.cloned.1.call-done) | copy-start | bytes 4718596
  396.2 41.0 %copy-start.1 = (bf16[32,3072]{1,0:T(8,128)(2,1)S(1)}, bf16[32,3072]{1,0:T(8,128)(2,1)}, u32[]{:S(2)}) copy-start(bf16[32,3072]{1,0:T(8,128)(2,1)} %param.12) | copy-start | bytes 589828
  396.2 42.1 %copy-start.3 = (f32[3072]{0:T(1024)S(1)}, f32[3072]{0:T(1024)}, u32[]{:S(2)}) copy-start(f32[3072]{0:T(1024)} %param.18) | copy-start | bytes 36868
  396.3 126.7 %all-gather.22.cloned.1.call-start = ((), (), s32[]{:S(2)}) async-start(), calls=%async_computation.9 | async-start | bytes 3194880 | tf_op jit(solution)/shard_map/all_gather | solution.py:101
  397.0 169.2 %all-gather.20.cloned.1.call-start = ((), (), s32[]{:S(2)}) async-start(), calls=%async_computation.8 | async-start | bytes 1769472 | tf_op jit(solution)/shard_map/all_gather | solution.py:97
  440.1 211.7 %all-gather.24.cloned.1.call-start = ((), (), s32[]{:S(2)}) async-start(), calls=%async_computation.10 | async-start | bytes 3194880 | tf_op jit(solution)/shard_map/all_gather | solution.py:102
  440.8 295.6 %all-gather.26.cloned.1.call-start = ((), (), s32[]{:S(2)}) async-start(), calls=%async_computation.11 | async-start | bytes 3194880 | tf_op jit(solution)/shard_map/all_gather | solution.py:108
  441.4 342.3 %reduce-scatter.5.cloned.1.call-start = ((), (), s32[]{:S(2)}) async-start(), calls=%async_computation.12 | async-start | bytes 1769472 | tf_op jit(solution)/shard_map/reduce_scatter | solution.py:111
  742.8 0.7 copy-start.4
  742.8 40.9 %copy-start.2 = (bf16[32,3072]{1,0:T(8,128)(2,1)S(1)}, bf16[32,3072]{1,0:T(8,128)(2,1)}, u32[]{:S(2)}) copy-start(bf16[32,3072]{1,0:T(8,128)(2,1)} %reduce-scatter.3.cloned.1.call-done) | copy-start | bytes 589828
Sparse Core Ops, SparseCore 0:
  11.3 86.7 all-gather.15
  100.8 40.5 all-gather.9
  144.8 81.1 all-gather.13
  229.1 80.3 all-gather.11
  312.7 80.3 all-gather.17
  396.4 40.8 reduce-scatter.2
  440.6 82.3 all-gather.21
  525.6 40.5 all-gather.19
  569.5 82.2 all-gather.23
  655.0 81.3 all-gather.25
  742.9 40.7 reduce-scatter.4
where the time goes:
time: 792 us
  waiting for transfers between devices  741 us (94%)
  matrix products  21 us (3%)
  between operations  14 us (2%)
  other arithmetic  9.76 us (1%)
    all_gather x1, waiting for transfers between devices, per_device(): lax.all_gather(w_down, 'group', axis=1, tiled=True)  84.6 us
    all_gather x1, waiting for transfers between devices, per_device(): lax.all_gather(w_key, 'group', axis=0, tiled=True)  82.9 us
    all_gather x1, waiting for transfers between devices, per_device(): lax.all_gather(w_up, 'group', axis=0, tiled=True)  82.3 us
    all_gather x1, waiting for transfers between devices, per_device(): lax.all_gather(w_query, 'group', axis=0, tiled=True)  81.7 us
    all_gather x1, waiting for transfers between devices, per_device(): lax.all_gather(w_gate, 'group', axis=0, tiled=True)  81.5 us
    all_gather x1, waiting for transfers between devices, per_device(): lax.all_gather(w_out, 'group', axis=1, tiled=True)  81.1 us
    all_gather x1, waiting for transfers between devices, per_device(): lax.all_gather(w_value, 'group', axis=0, tiled=True)  80.6 us
    all_gather x1, waiting for transfers between devices, per_device(): whole = lax.all_gather(normed, 'head', axis=0, tiled=True)  43.3 us
  transfers between devices with their start and end apart: 11, of which 11 were waited for; matrix products, arithmetic and copies ran while one was open for 3% of the time, Pallas kernels for 0%

commit v1 on v0

v1 whole, which is shorter than its diff:
```python
import jax
import jax.numpy as jnp
import numpy as np
from jax import lax
from jax.experimental import pallas as pl
from jax.experimental.pallas import tpu as pltpu
from jax.sharding import PartitionSpec as P

MESH = pl.DeviceIdType.MESH
F32, BF16 = jnp.float32, jnp.bfloat16
NX, NZ, NY = 4, 8, 8
HEAD_DIM = 96
HALF = HEAD_DIM // 2
LANES = 128


def wrap(value, add, count):
    return lax.rem(value + (add + count), count)


def iota(shape, dim):
    return lax.broadcasted_iota(jnp.int32, shape, dim)


def nn(left, right):
    return jnp.dot(left, right, preferred_element_type=F32)


def nt(left, right):
    return lax.dot_general(left, right, (((1,), (1,)), ((), ())), preferred_element_type=F32)


def norm_rows(values, gain):
    scale = lax.rsqrt(jnp.mean(values * values, axis=-1, keepdims=True) + 1e-05)
    return (values * scale * gain).astype(BF16)


class Net:
    def __init__(self, send, recv):
        self.send, self.recv, self.copies = send, recv, []

    def put(self, src, dst, device):
        k = len(self.copies)
        copy = pltpu.make_async_remote_copy(
            src_ref=src,
            dst_ref=dst,
            send_sem=self.send.at[k],
            recv_sem=self.recv.at[k],
            device_id=device,
            device_id_type=MESH,
        )
        copy.start()
        self.copies.append(copy)
        return copy

    def drain(self):
        for copy in self.copies:
            copy.wait_send()


class Place:
    def __init__(self):
        group = lax.axis_index("group")
        self.y = lax.axis_index("head")
        self.core = lax.rem(group, 2)
        self.z = lax.rem(lax.div(group, 2), NZ)
        self.x = lax.div(group, 2 * NZ)

    def index(self, dx, dz, core):
        return (wrap(self.x, dx, NX) * NZ + wrap(self.z, dz, NZ)) * 2 + core

    def device(self, dx=0, dz=0, dy=0, sibling=False):
        core = 1 - self.core if sibling else self.core
        return (self.index(dx, dz, core), wrap(self.y, dy, NY))

    def neighbours(self):
        return (
            self.device(dx=1),
            self.device(dx=-1),
            self.device(dz=1),
            self.device(dz=-1),
            self.device(dy=1),
            self.device(dy=-1),
            self.device(sibling=True),
        )


def gather_weights(net, at, whole, rows):
    def block(dx, dz):
        start = pl.multiple_of(at.index(dx, dz, at.core) * rows, rows)
        return whole.at[pl.ds(start, rows), :]

    def push(ref, **where):
        return net.put(ref, ref, at.device(**where))

    siblings, across, second = [], {}, {}
    order = [0, -1, 1, -2, 2, -3, 3, -4]

    def arrived(dz):
        ref = block(0, dz)
        across[dz] = (push(ref, dx=1), push(ref, dx=-1))
        siblings.append(push(ref, sibling=True))

    def cross(dz):
        onward = order.index(dz) % 2
        for side in (0, 1):
            across[dz][side].wait_recv()
            ref = block(-1 if side == 0 else 1, dz)
            if side == onward:
                second[dz] = push(ref, dx=1 if side == 0 else -1)
            siblings.append(push(ref, sibling=True))

    def last(dz):
        second[dz].wait_recv()
        siblings.append(push(block(2, dz), sibling=True))

    own = block(0, 0)
    up, down = push(own, dz=1), push(own, dz=-1)
    arrived(0)
    yield
    todo_cross, todo_last = [0], []
    for step in range(1, 5):
        up.wait_recv()
        if step < 4:
            up = push(block(0, -step), dz=1)
        arrived(-step)
        fresh = [-step]
        if step < 4:
            down.wait_recv()
            if step < 3:
                down = push(block(0, step), dz=-1)
            arrived(step)
            fresh.append(step)
        yield
        for dz in todo_cross:
            cross(dz)
        for dz in todo_last:
            last(dz)
        todo_cross, todo_last = fresh, todo_cross
        yield
    for dz in todo_cross:
        cross(dz)
    yield
    for dz in todo_last + todo_cross:
        last(dz)
    yield
    for copy in siblings:
        copy.wait_recv()


def ways(chunk):
    return (4, 3) if chunk % 2 == 0 else (3, 4)


def gather_rows(net, at, whole, rows, chunks):
    width = whole.shape[1] // chunks

    def block(dy, chunk):
        start = pl.multiple_of(wrap(at.y, dy, NY) * rows, rows)
        return whole.at[pl.ds(start, rows), pl.ds(chunk * width, width)]

    flight = {}
    for step in range(1, 5):
        for chunk in range(chunks):
            for way in (0, 1):
                sign = 1 if way == 0 else -1
                if step > ways(chunk)[way]:
                    continue
                if step > 1:
                    flight[chunk, way].wait_recv()
                ref = block(-sign * (step - 1), chunk)
                flight[chunk, way] = net.put(ref, ref, at.device(dy=sign))
        yield
    for copy in flight.values():
        copy.wait_recv()


def sum_rows(net, at, terms, held, rows, chunks, finish):
    width = terms.shape[1] // chunks
    flight = {}

    def term(dy, columns):
        start = pl.multiple_of(wrap(at.y, dy, NY) * rows, rows)
        return terms.at[pl.ds(start, rows), columns]

    for step in range(1, 5):
        for chunk in range(chunks):
            columns = pl.ds(chunk * width, width)
            for way in (0, 1):
                sign, length = (1 if way == 0 else -1), ways(chunk)[way]
                if step > length:
                    continue
                mine = term(sign * (length - step + 1), columns)
                if step > 1:
                    flight[chunk, way].wait_recv()
                    slot = held.at[way, step - 2, :, columns]
                    slot[...] = (slot[...].astype(F32) + mine[...].astype(F32)).astype(BF16)
                    mine = slot
                flight[chunk, way] = net.put(mine, held.at[way, step - 1, :, columns], at.device(dy=sign))
        yield
    for chunk in range(chunks):
        columns = pl.ds(chunk * width, width)
        total = term(0, columns)[...].astype(F32)
        for way in (0, 1):
            flight[chunk, way].wait_recv()
            total = total + held[way, ways(chunk)[way] - 1, :, columns].astype(F32)
        finish(columns, total)


def key_columns():
    row, col = iota((2 * LANES, 2 * HEAD_DIM), 0), iota((2 * LANES, 2 * HEAD_DIM), 1)
    second = row >= LANES
    lane = jnp.where(second, row - LANES, row)
    target = lane + jnp.where(lane >= HALF, HALF, 0) + jnp.where(second, HALF, 0)
    return jnp.where((target == col) & (lane < HEAD_DIM), 1.0, 0.0).astype(BF16)


def value_columns():
    row, col = iota((2 * LANES, 2 * HEAD_DIM), 0), iota((2 * LANES, 2 * HEAD_DIM), 1)
    second = row >= LANES
    lane = jnp.where(second, row - LANES, row)
    target = lane + jnp.where(second, HEAD_DIM, 0)
    return jnp.where((target == col) & (lane < HEAD_DIM), 1.0, 0.0).astype(BF16)


def spare_columns():
    row, col = iota((2 * HEAD_DIM, 6 * LANES), 0), iota((2 * HEAD_DIM, 6 * LANES), 1)
    tile, lane = lax.shift_right_logical(col, 7), lax.bitwise_and(col, LANES - 1)
    return jnp.where((lane >= HEAD_DIM) & (row == tile * 32 + lane - HEAD_DIM), 1.0, 0.0).astype(BF16)


def eye(size):
    return jnp.where(iota((size, size), 0) == iota((size, size), 1), 1.0, 0.0).astype(BF16)


def pack_attention(wq, wk, wv, wo, dest):
    keys, values = key_columns(), value_columns()
    turned = nt(eye(wo.shape[1]), wo[...]).astype(BF16)
    spare = nn(turned, spare_columns())
    main = jnp.concatenate([nt(wq[...], keys), nt(wk[...], keys), nt(wv[...], values)], axis=1)
    dest[...] = (main + spare).astype(BF16)


def attention(qkv, seg, slot, freq, ck, cv):
    count = qkv.shape[0]
    row, col = iota((count, count), 0), iota((count, count), 1)
    seg_k = jnp.broadcast_to(seg[...], (count, count))
    seg_q = jnp.sum(jnp.where(row == col, seg_k, 0.0), axis=1, keepdims=True)
    first = jnp.sum(jnp.where(seg_k < seg_q, 1.0, 0.0), axis=1, keepdims=True)
    place = iota((count, 1), 0).astype(F32) - first
    angle = place * freq[...]
    cosine, sine = jnp.cos(angle), jnp.sin(angle)
    lane = iota((count, LANES), 1)
    live = lane < HEAD_DIM

    def tile(k):
        return qkv[:, k * LANES : (k + 1) * LANES]

    def rotated(u, w):
        turned = (u * cosine - w * sine, w * cosine + u * sine)
        return [jnp.where(live, part, 0.0).astype(BF16) for part in turned]

    queries = jnp.concatenate(rotated(tile(0), tile(1)), axis=1)
    key_parts = rotated(tile(2), tile(3))
    keys = jnp.concatenate(key_parts, axis=1)
    values = [jnp.where(live, tile(k), 0.0).astype(BF16) for k in (4, 5)]
    to_slot = jnp.where(row == jnp.broadcast_to(slot[...], (count, count)), 1.0, 0.0).astype(BF16)
    ck[...] = nn(nn(to_slot, keys).astype(BF16), key_columns()).astype(BF16)
    cv[...] = nn(nn(to_slot, jnp.concatenate(values, axis=1)).astype(BF16), value_columns()).astype(BF16)
    allowed = (seg_k == seg_q) & (col <= row)
    mixed = []
    for head in (0, 1):
        of_head = (lane >= head * HALF) & (lane < (head + 1) * HALF)
        key = jnp.concatenate([jnp.where(of_head, part, jnp.zeros_like(part)) for part in key_parts], axis=1)
        scores = nt(queries, key) * (1.0 / HEAD_DIM**0.5)
        scores = jnp.where(allowed, scores, -1e30)
        expo = jnp.exp(scores - jnp.max(scores, axis=1, keepdims=True))
        probs = (expo / jnp.sum(expo, axis=1, keepdims=True)).astype(BF16)
        mixed.append(nn(probs, values[head]).astype(BF16))
    return nn(jnp.concatenate(mixed, axis=1), value_columns()).astype(BF16)


def layer(
    tokens, gain, wq, wk, wv, wo, gain2, wg, wu, wd, seg, slot, freq,
    out, ck, cv,
    wa, wb, normed, normed2, qkv, spread, terms, terms2, hidden, held, held2, middle, send, recv,
):
    at = Place()
    net = Net(send, recv)
    rows, width = tokens.shape
    part, units = wq.shape[0], wg.shape[1]
    step = 256

    barrier = pltpu.get_barrier_semaphore()
    for device in at.neighbours():
        pl.semaphore_signal(barrier, inc=1, device_id=device, device_id_type=MESH)

    mine = pl.ds(pl.multiple_of(at.y * rows, rows), rows)
    shard = pl.ds(pl.multiple_of(at.index(0, 0, at.core) * part, part), part)
    normed[mine, :] = norm_rows(tokens[...].astype(F32), gain[...])
    pack_attention(wq, wk, wv, wo, wa.at[shard, :])
    pl.semaphore_wait(barrier, 7)

    weights = gather_weights(net, at, wa, part)
    for _ in gather_rows(net, at, normed, rows, 2):
        next(weights, None)
        next(weights, None)
    for _ in weights:
        pass

    wb[shard, pl.ds(0, units)] = wg[...]
    wb[shard, pl.ds(units, units)] = wu[...]
    wb[shard, pl.ds(2 * units, units)] = nt(eye(part), wd[...]).astype(BF16)
    weights = gather_weights(net, at, wb, part)
    next(weights)

    def project(k, carry):
        columns = pl.ds(pl.multiple_of(k * step, step), step)
        qkv[:, columns] = nn(normed[...], wa[:, columns])
        return carry

    lax.fori_loop(0, qkv.shape[1] // step, project, 0)
    next(weights)
    attended = attention(qkv, seg, slot, freq, ck, cv)
    spread[...] = nn(attended, spare_columns()).astype(BF16)

    def expand(k, carry):
        columns = pl.ds(pl.multiple_of(k * step, step), step)
        terms[:, columns] = nt(spread[...], wa[columns, :]).astype(BF16)
        return carry

    lax.fori_loop(0, width // step, expand, 0)
    next(weights)

    def add_attention(columns, total):
        middle[:, columns] = (tokens[:, columns].astype(F32) + total).astype(BF16)

    for _ in sum_rows(net, at, terms, held, rows, 2, add_attention):
        next(weights, None)
    normed2[mine, :] = norm_rows(middle[...].astype(F32), gain2[...])
    for _ in gather_rows(net, at, normed2, rows, 2):
        next(weights, None)
    for _ in weights:
        pass

    def gated(k, carry):
        first = pl.ds(pl.multiple_of(k * step, step), step)
        later = pl.ds(pl.multiple_of(k * step + units, step), step)
        gate = nn(normed2[...], wb[:, first])
        up = nn(normed2[...], wb[:, later])
        hidden[:, first] = (gate / (1.0 + jnp.exp(-gate)) * up).astype(BF16)
        return carry

    lax.fori_loop(0, units // step, gated, 0)

    def lower(k, carry):
        columns = pl.ds(pl.multiple_of(k * step, step), step)
        terms2[:, columns] = nt(hidden[...], wb[columns, pl.ds(2 * units, units)]).astype(BF16)
        return carry

    lax.fori_loop(0, width // step, lower, 0)

    def add_mlp(columns, total):
        out[:, columns] = (middle[:, columns].astype(F32) + total).astype(BF16)

    for _ in sum_rows(net, at, terms2, held2, rows, 2, add_mlp):
        pass
    net.drain()


def frequencies():
    lane = np.arange(LANES) % HALF
    return (10000.0 ** (-2.0 * lane / HEAD_DIM)).astype(np.float32)[None, :]


def per_device(
    tokens, attn_gain, w_query, w_key, w_value, w_out, mlp_gain, w_gate, w_up, w_down, segment_ids, cache_slot
):
    rows, width = tokens.shape
    heads = w_query.shape[1]
    units = w_gate.shape[1]
    count = rows * NY
    copies = 2 * 63 + 4 * 14
    vmem = pl.BlockSpec(memory_space=pltpu.VMEM)
    return pl.pallas_call(
        layer,
        name="layer",
        out_shape=(
            jax.ShapeDtypeStruct((rows, width), BF16),
            jax.ShapeDtypeStruct((count, heads), BF16),
            jax.ShapeDtypeStruct((count, heads), BF16),
        ),
        in_specs=[vmem] * 13,
        out_specs=(vmem,) * 3,
        scratch_shapes=[
            pltpu.VMEM((width, 6 * LANES), BF16),
            pltpu.VMEM((width, 3 * units), BF16),
            pltpu.VMEM((count, width), BF16),
            pltpu.VMEM((count, width), BF16),
            pltpu.VMEM((count, 6 * LANES), F32),
            pltpu.VMEM((count, 6 * LANES), BF16),
            pltpu.VMEM((count, width), BF16),
            pltpu.VMEM((count, width), BF16),
            pltpu.VMEM((count, units), BF16),
            pltpu.VMEM((2, 4, rows, width), BF16),
            pltpu.VMEM((2, 4, rows, width), BF16),
            pltpu.VMEM((rows, width), BF16),
            pltpu.SemaphoreType.DMA((copies,)),
            pltpu.SemaphoreType.DMA((copies,)),
        ],
        compiler_params=pltpu.CompilerParams(
            collective_id=0, has_side_effects=True, vmem_limit_bytes=56 * 2**20
        ),
    )(
        tokens,
        attn_gain[None, :],
        w_query,
        w_key,
        w_value,
        w_out,
        mlp_gain[None, :],
        w_gate,
        w_up,
        w_down,
        segment_ids.astype(F32),
        cache_slot,
        jnp.asarray(frequencies()),
    )


def solution(mesh):
    in_specs = (
        P(("group", "head"), None),
        P(),
        P("group", "head"),
        P("group", "head"),
        P("group", "head"),
        P("head", "group"),
        P(),
        P("group", "head"),
        P("group", "head"),
        P("head", "group"),
        P("group", None),
        P("group", None),
    )
    out_specs = (P(("group", "head"), None), P("group", "head"), P("group", "head"))
    return jax.shard_map(
        per_device, mesh=mesh, in_specs=in_specs, out_specs=out_specs, check_vma=False
    )
```

time: 792 us -> 126 us (0.16)
  waiting for transfers between devices: 741 us -> 0 us
  Pallas kernels: 0 us -> 118 us
  matrix products: 21 us -> 0 us
  between operations: 14 us -> 0.67 us
  other arithmetic: 9.76 us -> 1.26 us
    all_gather x9 -> x0, waiting for transfers between devices: 661 us -> none  [the longest x1 84.6 us: per_device(): lax.all_gather(w_down, 'group', axis=1, tiled=True)]
    pallas_call x0 -> x1, Pallas kernels: none -> 118 us  [per_device(): pl.pallas_call(layer, name='layer', out_shape=(jax.ShapeDtypeStruct((rows...]
    reduce_scatter x2 -> x0, waiting for transfers between devices: 75.7 us -> none  [the longest x1 40.2 us: per_device(): lax.psum_scatter(out_terms.astype(jnp.bfloat16), 'head', scatter_dimensio...]
    dot_general x8 -> x0, matrix products: 20.6 us -> none  [the longest x4 10.5 us: accumulate(): jnp.dot(source, piece, preferred_element_type=jnp.float32)]
  transfers between devices with their start and end apart: 11 -> 0, of which waited for: 11 -> 0; matrix products, arithmetic and copies ran while one was open for 3% -> 0% of each run, Pallas kernels for 0% -> 0%
where the time goes in v1:
time: 126 us
  Pallas kernels  118 us (94%)
  local copies, waits for them, and re-layouts  5.35 us (4%)
  other arithmetic  1.26 us (1%)
    pallas_call x1, Pallas kernels, per_device(): pl.pallas_call(layer, name='layer', out_shape=(jax.ShapeDtypeStruct((rows...  118 us
    unnamed x9, local copies, waits for them, and re-layouts  2.91 us

profile of v1, /device:TPU:6, one launch (start us, length us, event | category | flops | bytes accessed | tf_op | source)
XLA Modules:
  0.0 125.8 jit_solution(15608278367725110117)
XLA Ops:
  0.6 0.0 copy-start.2
  0.6 1.3 convert_element_type.3.seg
  1.9 1.5 %copy.16.wo = bf16[192,48]{1,0:T(8,128)(2,1)} copy(bf16[192,48]{0,1:T(8,128)(2,1)} %param.18) | data formatting | bytes 36864 | tf_op args[5]
  3.4 0.0 copy-done.2
  3.4 0.8 copy.17.wd
  4.1 118.5 %layer.1 = (bf16[32,3072]{1,0:T(8,128)(2,1)}, bf16[256,192]{1,0:T(8,128)(2,1)}, bf16[256,192]{1,0:T(8,128)(2,1)}) custom-call(bf16[32,3072]{1,0:T(8,128)(2,1)} %tokens.1, f32[1,3072]{1,0:T(1,128)} %bitcast.2, bf16[48,192]{1,0:T(8,128)(2,1)} %wq.1, bf16[48,192]{1,0:T(8,128)(2,1)} %wk.1, bf16[48,192]{1,0:T(8,128)(2,1)} %wv.1, bf16[192,48]{1,0:T(8,128)(2,1)} %copy.16.wo, ...), custom_call_target="tpu_custom_call" | custom-call | tf_op jit(solution)/shard_map/layer/pallas_call | solution.py:385
  122.6 0.0 copy-start.1
  122.6 0.0 copy-start
  122.6 1.7 %copy.18 = bf16[256,192]{0,1:T(8,128)(2,1)} copy(bf16[256,192]{1,0:T(8,128)(2,1)} %get-tuple-element.4) | data formatting | bytes 196608 | tf_op jit(solution)/shard_map/layer/pallas_call | solution.py:385
  124.3 0.0 copy-done.1
  124.3 0.7 copy.19
  125.1 0.0 copy-done
  125.1 0.7 copy.21
Async XLA Ops:
  0.6 2.7 %copy-start.2 = (bf16[512,48]{0,1:T(8,128)(2,1)S(1)}, bf16[512,48]{0,1:T(8,128)(2,1)}, u32[]{:S(2)}) copy-start(bf16[512,48]{0,1:T(8,128)(2,1)} %param.22) | copy-start | bytes 147460
  122.6 1.7 %copy-start.1 = (bf16[256,192]{1,0:T(8,128)(2,1)S(1)}, bf16[256,192]{1,0:T(8,128)(2,1)}, u32[]{:S(2)}) copy-start(bf16[256,192]{1,0:T(8,128)(2,1)} %get-tuple-element.5) | copy-start | bytes 294916
  122.6 2.5 %copy-start = (bf16[32,3072]{1,0:T(8,128)(2,1)S(1)}, bf16[32,3072]{1,0:T(8,128)(2,1)}, u32[]{:S(2)}) copy-start(bf16[32,3072]{1,0:T(8,128)(2,1)} %get-tuple-element.9) | copy-start | bytes 589828

commit v2 on v1

v2 whole, which is shorter than its diff:
```python
import jax
import jax.numpy as jnp
import numpy as np
from jax import lax
from jax.experimental import pallas as pl
from jax.experimental.pallas import tpu as pltpu
from jax.sharding import PartitionSpec as P

MESH = pl.DeviceIdType.MESH
F32, BF16 = jnp.float32, jnp.bfloat16
NX, NZ, NY = 4, 8, 8
HEAD_DIM = 96
HALF = HEAD_DIM // 2
LANES = 128


def wrap(value, add, count):
    return lax.rem(value + (add + count), count)


def iota(shape, dim):
    return lax.broadcasted_iota(jnp.int32, shape, dim)


def nn(left, right):
    return jnp.dot(left, right, preferred_element_type=F32)


def nt(left, right):
    return lax.dot_general(left, right, (((1,), (1,)), ((), ())), preferred_element_type=F32)


def norm_rows(values, gain):
    scale = lax.rsqrt(jnp.mean(values * values, axis=-1, keepdims=True) + 1e-05)
    return (values * scale * gain).astype(BF16)


class Net:
    def __init__(self, send, recv):
        self.send, self.recv, self.count = send, recv, 0

    def put(self, src, dst, device, k=None):
        if k is None:
            k, self.count = self.count, self.count + 1
        copy = pltpu.make_async_remote_copy(
            src_ref=src,
            dst_ref=dst,
            send_sem=self.send,
            recv_sem=self.recv.at[k],
            device_id=device,
            device_id_type=MESH,
        )
        copy.start()
        return copy

    def landed(self, ref, k, device):
        pltpu.make_async_remote_copy(ref, ref, self.send, self.recv.at[k], device, MESH).wait_recv()

    def sent(self, ref, device):
        pltpu.make_async_remote_copy(ref, ref, self.send, self.recv.at[0], device, MESH).wait_send()


class Place:
    def __init__(self):
        group = lax.axis_index("group")
        self.y = lax.axis_index("head")
        self.core = lax.rem(group, 2)
        self.z = lax.rem(lax.div(group, 2), NZ)
        self.x = lax.div(group, 2 * NZ)

    def index(self, dx, dz, core):
        return (wrap(self.x, dx, NX) * NZ + wrap(self.z, dz, NZ)) * 2 + core

    def device(self, dx=0, dz=0, dy=0, sibling=False):
        core = 1 - self.core if sibling else self.core
        return (self.index(dx, dz, core), wrap(self.y, dy, NY))

    def neighbours(self):
        return (
            self.device(dx=1),
            self.device(dx=-1),
            self.device(dz=1),
            self.device(dz=-1),
            self.device(dy=1),
            self.device(dy=-1),
            self.device(sibling=True),
        )


def route(first):
    blocks = []
    for dx in (0, -1, 1, 2):
        up = 4 if first == "z" or dx in (0, 2) else 3
        for dz in range(-up, NZ - up):
            on = []
            if first == "x" or dx == 0:
                if dz <= 0 and -dz < up:
                    on.append((0, 1))
                if dz >= 0 and dz < NZ - 1 - up:
                    on.append((0, -1))
            if first == "z" or dz == 0:
                if dx == 0:
                    on += [(1, 0), (-1, 0)]
                elif dx == -1 and (first == "x" or dz % 2 == 0):
                    on.append((1, 0))
                elif dx == 1 and first == "z" and dz % 2 == 1:
                    on.append((-1, 0))
            later = abs(dx) if first == "z" else abs(dz)
            blocks.append(((abs(dx) + abs(dz), later), dx, dz, on))
    return [block[1:] for block in sorted(blocks, key=lambda block: block[0])]


def gather_weights(net, at, whole, rows):
    def block(dx, dz):
        start = pl.multiple_of(at.index(dx, dz, at.core) * rows, rows)
        return whole.at[pl.ds(start, rows), :]

    def name(dx, dz):
        return (dx % NX) * NZ + dz % NZ

    other = NX * NZ

    def handle(dx, dz, on):
        ref = block(dx, dz)
        if (dx, dz) != (0, 0):
            net.landed(ref, name(dx, dz), at.device(dx=1))
        for sx, sz in on:
            net.put(ref, ref, at.device(dx=sx, dz=sz), name(dx - sx, dz - sz))
        net.put(ref, ref, at.device(sibling=True), other)

    for pair in zip(route("z"), route("x")):
        for core in (0, 1):

            @pl.when(at.core == core)
            def _(todo=pair[core]):
                handle(*todo)

        yield
    count = whole.shape[0]
    net.landed(whole.at[pl.ds(0, count // 2), :], other, at.device(sibling=True))
    net.sent(whole.at[pl.ds(0, count - rows), :], at.device(sibling=True))


def ways(chunk):
    return (4, 3) if chunk % 2 == 0 else (3, 4)


def gather_rows(net, at, whole, rows, chunks):
    width = whole.shape[1] // chunks

    def block(dy, chunk):
        start = pl.multiple_of(wrap(at.y, dy, NY) * rows, rows)
        return whole.at[pl.ds(start, rows), pl.ds(chunk * width, width)]

    flight = {}
    for step in range(1, 5):
        for chunk in range(chunks):
            for way in (0, 1):
                sign = 1 if way == 0 else -1
                if step > ways(chunk)[way]:
                    continue
                if step > 1:
                    flight[chunk, way].wait_recv()
                ref = block(-sign * (step - 1), chunk)
                flight[chunk, way] = net.put(ref, ref, at.device(dy=sign))
            yield
    for copy in flight.values():
        copy.wait_recv()
    net.sent(whole.at[pl.ds(0, (NY - 1) * rows), :], at.device(dy=1))


def sum_rows(net, at, terms, held, rows, chunks, produce, consume):
    width = terms.shape[1] // chunks
    flight = {}

    def term(dy, columns):
        start = pl.multiple_of(wrap(at.y, dy, NY) * rows, rows)
        return terms.at[pl.ds(start, rows), columns]

    for step in range(1, 5):
        for chunk in range(chunks):
            columns = pl.ds(chunk * width, width)
            if step == 1:
                produce(chunk * width, width)
            for way in (0, 1):
                sign, length = (1 if way == 0 else -1), ways(chunk)[way]
                if step > length:
                    continue
                mine = term(sign * (length - step + 1), columns)
                if step > 1:
                    flight[chunk, way].wait_recv()
                    slot = held.at[way, step - 2, :, columns]
                    slot[...] = (slot[...].astype(F32) + mine[...].astype(F32)).astype(BF16)
                    mine = slot
                flight[chunk, way] = net.put(mine, held.at[way, step - 1, :, columns], at.device(dy=sign))
            yield
    for chunk in range(chunks):
        columns = pl.ds(chunk * width, width)
        total = term(0, columns)[...].astype(F32)
        for way in (0, 1):
            flight[chunk, way].wait_recv()
            total = total + held[way, ways(chunk)[way] - 1, :, columns].astype(F32)
        consume(columns, total)
        yield
    net.sent(terms.at[pl.ds(0, (NY - 1) * rows), :], at.device(dy=1))


def weave(main, side, each):
    for k, _ in enumerate(main):
        if k % each == each - 1:
            next(side, None)


def finish(steps):
    for _ in steps:
        pass


def key_columns():
    row, col = iota((2 * HEAD_DIM, 2 * LANES), 0), iota((2 * HEAD_DIM, 2 * LANES), 1)
    second = col >= LANES
    lane = jnp.where(second, col - LANES, col)
    source = lane + jnp.where(lane >= HALF, HALF, 0) + jnp.where(second, HALF, 0)
    return jnp.where((source == row) & (lane < HEAD_DIM), 1.0, 0.0).astype(BF16)


def value_columns():
    row, col = iota((2 * HEAD_DIM, 2 * LANES), 0), iota((2 * HEAD_DIM, 2 * LANES), 1)
    second = col >= LANES
    lane = jnp.where(second, col - LANES, col)
    source = lane + jnp.where(second, HEAD_DIM, 0)
    return jnp.where((source == row) & (lane < HEAD_DIM), 1.0, 0.0).astype(BF16)


def spare_columns():
    row, col = iota((2 * HEAD_DIM, 6 * LANES), 0), iota((2 * HEAD_DIM, 6 * LANES), 1)
    tile, lane = lax.shift_right_logical(col, 7), lax.bitwise_and(col, LANES - 1)
    return jnp.where((lane >= HEAD_DIM) & (row == tile * 32 + lane - HEAD_DIM), 1.0, 0.0).astype(BF16)


def pack_attention(wq, wk, wv, wo, dest):
    keys, values = key_columns(), value_columns()
    spare = nn(wo[...], spare_columns())
    main = jnp.concatenate([nn(wq[...], keys), nn(wk[...], keys), nn(wv[...], values)], axis=1)
    dest[...] = (main + spare).astype(BF16)


def attention(qkv, seg, slot, freq, ck, cv):
    count = qkv.shape[0]
    row, col = iota((count, count), 0), iota((count, count), 1)
    seg_k = jnp.broadcast_to(seg[...].astype(F32), (count, count))
    seg_q = jnp.sum(jnp.where(row == col, seg_k, 0.0), axis=1, keepdims=True)
    first = jnp.sum(jnp.where(seg_k < seg_q, 1.0, 0.0), axis=1, keepdims=True)
    place = iota((count, 1), 0).astype(F32) - first
    angle = place * freq[...]
    cosine, sine = jnp.cos(angle), jnp.sin(angle)
    lane = iota((count, LANES), 1)
    live = lane < HEAD_DIM

    def tile(k):
        return qkv[:, k * LANES : (k + 1) * LANES]

    def rotated(u, w):
        turned = (u * cosine - w * sine, w * cosine + u * sine)
        return [jnp.where(live, part, 0.0).astype(BF16) for part in turned]

    queries = jnp.concatenate(rotated(tile(0), tile(1)), axis=1)
    key_parts = rotated(tile(2), tile(3))
    keys = jnp.concatenate(key_parts, axis=1)
    values = [jnp.where(live, tile(k), 0.0).astype(BF16) for k in (4, 5)]
    to_slot = jnp.where(row == jnp.broadcast_to(slot[...], (count, count)), 1.0, 0.0).astype(BF16)
    ck[...] = nt(key_columns(), nn(to_slot, keys).astype(BF16)).astype(BF16)
    cv[...] = nt(value_columns(), nn(to_slot, jnp.concatenate(values, axis=1)).astype(BF16)).astype(BF16)
    allowed = (seg_k == seg_q) & (col <= row)
    mixed = []
    for head in (0, 1):
        of_head = (lane >= head * HALF) & (lane < (head + 1) * HALF)
        key = jnp.concatenate([jnp.where(of_head, part, jnp.zeros_like(part)) for part in key_parts], axis=1)
        scores = nt(queries, key) * (1.0 / HEAD_DIM**0.5)
        scores = jnp.where(allowed, scores, -1e30)
        expo = jnp.exp(scores - jnp.max(scores, axis=1, keepdims=True))
        probs = (expo / jnp.sum(expo, axis=1, keepdims=True)).astype(BF16)
        mixed.append(nn(probs, values[head]).astype(BF16))
    return nt(jnp.concatenate(mixed, axis=1), value_columns()).astype(BF16)


def layer(
    tokens, gain, wq, wk, wv, wo, gain2, wg, wu, wd, seg, slot, freq,
    out, ck, cv,
    wa, wb, normed, normed2, qkv, spread, terms, terms2, hidden, held, held2, middle, send, recv_w, recv_y,
):
    at = Place()
    rows, width = tokens.shape
    part, units = wq.shape[0], wg.shape[1]
    step, chunks = 256, 4
    nets = [Net(send.at[k], recv_w.at[k]) for k in range(2)] + [Net(send.at[2 + k], recv_y.at[k]) for k in range(4)]

    barrier = pltpu.get_barrier_semaphore()
    for device in at.neighbours():
        pl.semaphore_signal(barrier, inc=1, device_id=device, device_id_type=MESH)

    mine = pl.ds(pl.multiple_of(at.y * rows, rows), rows)
    shard = pl.ds(pl.multiple_of(at.index(0, 0, at.core) * part, part), part)
    normed[mine, :] = norm_rows(tokens[...].astype(F32), gain[...])
    pack_attention(wq, wk, wv, wo, wa.at[shard, :])
    wb[shard, pl.ds(0, units)] = wg[...]
    wb[shard, pl.ds(units, units)] = wu[...]
    wb[shard, pl.ds(2 * units, units)] = wd[...]
    pl.semaphore_wait(barrier, 7)

    weights = gather_weights(nets[0], at, wa, part)
    next(weights)
    weave(gather_rows(nets[2], at, normed, rows, chunks), weights, 1)
    finish(weights)

    weights = gather_weights(nets[1], at, wb, part)
    next(weights)

    def project(k, carry):
        columns = pl.ds(pl.multiple_of(k * step, step), step)
        qkv[:, columns] = nn(normed[...], wa[:, columns])
        return carry

    lax.fori_loop(0, qkv.shape[1] // step, project, 0)
    for _ in range(4):
        next(weights)
    attended = attention(qkv, seg, slot, freq, ck, cv)
    spread[...] = nn(attended, spare_columns()).astype(BF16)
    for _ in range(4):
        next(weights)

    def expand(start, size):
        def tile(k, carry):
            columns = pl.ds(pl.multiple_of(start + k * step, step), step)
            terms[:, columns] = nt(spread[...], wa[columns, :]).astype(BF16)
            return carry

        lax.fori_loop(0, size // step, tile, 0)

    def add_attention(columns, total):
        middle[:, columns] = (tokens[:, columns].astype(F32) + total).astype(BF16)

    weave(sum_rows(nets[3], at, terms, held, rows, chunks, expand, add_attention), weights, 2)
    normed2[mine, :] = norm_rows(middle[...].astype(F32), gain2[...])
    weave(gather_rows(nets[4], at, normed2, rows, chunks), weights, 1)
    finish(weights)

    def gated(k, carry):
        first = pl.ds(pl.multiple_of(k * step, step), step)
        later = pl.ds(pl.multiple_of(k * step + units, step), step)
        gate = nn(normed2[...], wb[:, first])
        up = nn(normed2[...], wb[:, later])
        hidden[:, first] = (gate / (1.0 + jnp.exp(-gate)) * up).astype(BF16)
        return carry

    lax.fori_loop(0, units // step, gated, 0)

    def lower(start, size):
        def tile(k, carry):
            columns = pl.ds(pl.multiple_of(start + k * step, step), step)
            terms2[:, columns] = nt(hidden[...], wb[columns, pl.ds(2 * units, units)]).astype(BF16)
            return carry

        lax.fori_loop(0, size // step, tile, 0)

    def add_mlp(columns, total):
        out[:, columns] = (middle[:, columns].astype(F32) + total).astype(BF16)

    finish(sum_rows(nets[5], at, terms2, held2, rows, chunks, lower, add_mlp))


def frequencies():
    lane = np.arange(LANES) % HALF
    return (10000.0 ** (-2.0 * lane / HEAD_DIM)).astype(np.float32)[None, :]


def per_device(
    tokens, attn_gain, w_query, w_key, w_value, w_out, mlp_gain, w_gate, w_up, w_down, segment_ids, cache_slot
):
    rows, width = tokens.shape
    heads = w_query.shape[1]
    units = w_gate.shape[1]
    count = rows * NY
    vmem = pl.BlockSpec(memory_space=pltpu.VMEM)
    layer_out, keys, values = pl.pallas_call(
        layer,
        name="layer",
        out_shape=(
            jax.ShapeDtypeStruct((rows, width), BF16),
            jax.ShapeDtypeStruct((heads, count), BF16),
            jax.ShapeDtypeStruct((heads, count), BF16),
        ),
        in_specs=[vmem] * 13,
        out_specs=(vmem,) * 3,
        scratch_shapes=[
            pltpu.VMEM((width, 6 * LANES), BF16),
            pltpu.VMEM((width, 3 * units), BF16),
            pltpu.VMEM((count, width), BF16),
            pltpu.VMEM((count, width), BF16),
            pltpu.VMEM((count, 6 * LANES), F32),
            pltpu.VMEM((count, 6 * LANES), BF16),
            pltpu.VMEM((count, width), BF16),
            pltpu.VMEM((count, width), BF16),
            pltpu.VMEM((count, units), BF16),
            pltpu.VMEM((2, 4, rows, width), BF16),
            pltpu.VMEM((2, 4, rows, width), BF16),
            pltpu.VMEM((rows, width), BF16),
            pltpu.SemaphoreType.DMA((6,)),
            pltpu.SemaphoreType.DMA((2, NX * NZ + 1)),
            pltpu.SemaphoreType.DMA((4, 28)),
        ],
        compiler_params=pltpu.CompilerParams(
            collective_id=0, has_side_effects=True, vmem_limit_bytes=56 * 2**20
        ),
    )(
        tokens,
        attn_gain[None, :],
        w_query,
        w_key,
        w_value,
        w_out.T,
        mlp_gain[None, :],
        w_gate,
        w_up,
        w_down.T,
        segment_ids,
        cache_slot,
        jnp.asarray(frequencies()),
    )
    return layer_out, keys.T, values.T


def solution(mesh):
    in_specs = (
        P(("group", "head"), None),
        P(),
        P("group", "head"),
        P("group", "head"),
        P("group", "head"),
        P("head", "group"),
        P(),
        P("group", "head"),
        P("group", "head"),
        P("head", "group"),
        P("group", None),
        P("group", None),
    )
    out_specs = (P(("group", "head"), None), P("group", "head"), P("group", "head"))
    return jax.shard_map(
        per_device, mesh=mesh, in_specs=in_specs, out_specs=out_specs, check_vma=False
    )
```

time: 126 us -> 120 us (0.952)
  Pallas kernels: 118 us -> 115 us
  local copies, waits for them, and re-layouts: 5.35 us -> 3.22 us
  other arithmetic: 1.26 us -> 0 us
    pallas_call x1, Pallas kernels: 118 us -> 115 us  [per_device(): pl.pallas_call(layer, name='layer', out_shape=(jax.ShapeDtypeStruct((rows...]
    pallas_call x2 -> x0, local copies, waits for them, and re-layouts: 2.44 us -> none  [per_device(): pl.pallas_call(layer, name='layer', out_shape=(jax.ShapeDtypeStruct((rows...]
    unnamed x9 -> x7, local copies, waits for them, and re-layouts: 2.91 us -> 3.22 us
where the time goes in v2:
time: 120 us; the launch traced here: 119 us
  Pallas kernels  115 us (96%)
  local copies, waits for them, and re-layouts  3.22 us (3%)
    pallas_call x1, Pallas kernels, per_device(): pl.pallas_call(layer, name='layer', out_shape=(jax.ShapeDtypeStruct((rows...  115 us
    unnamed x7, local copies, waits for them, and re-layouts  3.22 us

profile of v2, /device:TPU:6, one launch (start us, length us, event | category | flops | bytes accessed | tf_op | source)
XLA Modules:
  0.0 118.8 jit_solution(16156064859078727927)
XLA Ops:
  0.6 114.9 %layer.1 = (bf16[32,3072]{1,0:T(8,128)(2,1)}, bf16[192,256]{1,0:T(8,128)(2,1)}, bf16[192,256]{1,0:T(8,128)(2,1)}) custom-call(bf16[32,3072]{1,0:T(8,128)(2,1)} %tokens.1, f32[1,3072]{1,0:T(1,128)} %bitcast.10, bf16[48,192]{1,0:T(8,128)(2,1)} %wq.1, bf16[48,192]{1,0:T(8,128)(2,1)} %wk.1, bf16[48,192]{1,0:T(8,128)(2,1)} %wv.1, bf16[48,192]{1,0:T(8,128)(2,1)} %bitcast.9, ...), custom_call_target="tpu_custom_call" | custom-call | tf_op jit(solution)/shard_map/layer/pallas_call | solution.py:385
  115.6 0.0 copy-start.1
  115.6 1.6 %copy.19 = bf16[32,3072]{1,0:T(8,128)(2,1)} copy(bf16[32,3072]{1,0:T(8,128)(2,1)} %get-tuple-element.12) | data formatting | bytes 393216
  117.2 0.0 copy-done.1
  117.2 0.0 copy-start
  117.2 0.6 copy.20
  117.9 0.3 copy-done
  118.2 0.6 copy.21
Async XLA Ops:
  115.6 1.7 %copy-start.1 = (bf16[192,256]{1,0:T(8,128)(2,1)S(1)}, bf16[192,256]{1,0:T(8,128)(2,1)}, u32[]{:S(2)}) copy-start(bf16[192,256]{1,0:T(8,128)(2,1)} %get-tuple-element.7) | copy-start | bytes 294916
  117.2 0.9 copy-start

commit v3 on v2

--- a/solution.py
+++ b/solution.py
@@ -81,36 +81,47 @@
             self.device(dx=-1),
             self.device(dz=1),
             self.device(dz=-1),
+            self.device(dx=2),
+            self.device(dz=2),
+            self.device(dz=-2),
             self.device(dy=1),
             self.device(dy=-1),
             self.device(sibling=True),
         )
 
 
-def route(first):
+def route(first, far):
     blocks = []
     for dx in (0, -1, 1, 2):
         up = 4 if first == "z" or dx in (0, 2) else 3
         for dz in range(-up, NZ - up):
             on = []
-            if first == "x" or dx == 0:
+            if first == "z":
+                if dx == 0:
+                    if far:
+                        on += {0: [(0, 1), (0, -1), (0, 2), (0, -2)], -2: [(0, 2), (0, 1)], 2: [(0, -1)]}.get(dz, [])
+                    else:
+                        on += [(0, 1)] * (-4 < dz <= 0) + [(0, -1)] * (0 <= dz < 3)
+                    on += [(1, 0), (-1, 0)]
+                elif dx == -1 and dz % 2 == 0:
+                    on.append((1, 0))
+                elif dx == 1 and dz % 2 == 1:
+                    on.append((-1, 0))
+                depth = ((abs(dz) + 1) // 2 if far else abs(dz)) + abs(dx)
+            else:
+                if (dx, dz) == (0, 0):
+                    on += [(1, 0), (-1, 0), (2, 0)]
                 if dz <= 0 and -dz < up:
                     on.append((0, 1))
                 if dz >= 0 and dz < NZ - 1 - up:
                     on.append((0, -1))
-            if first == "z" or dz == 0:
-                if dx == 0:
-                    on += [(1, 0), (-1, 0)]
-                elif dx == -1 and (first == "x" or dz % 2 == 0):
-                    on.append((1, 0))
-                elif dx == 1 and first == "z" and dz % 2 == 1:
-                    on.append((-1, 0))
+                depth = (abs(dx) + 1) // 2 + abs(dz)
             later = abs(dx) if first == "z" else abs(dz)
-            blocks.append(((abs(dx) + abs(dz), later), dx, dz, on))
+            blocks.append(((depth, later), dx, dz, on))
     return [block[1:] for block in sorted(blocks, key=lambda block: block[0])]
 
 
-def gather_weights(net, at, whole, rows):
+def gather_weights(net, at, whole, rows, far):
     def block(dx, dz):
         start = pl.multiple_of(at.index(dx, dz, at.core) * rows, rows)
         return whole.at[pl.ds(start, rows), :]
@@ -128,7 +139,7 @@
             net.put(ref, ref, at.device(dx=sx, dz=sz), name(dx - sx, dz - sz))
         net.put(ref, ref, at.device(sibling=True), other)
 
-    for pair in zip(route("z"), route("x")):
+    for pair in zip(route("z", far), route("x", far)):
         for core in (0, 1):
 
             @pl.when(at.core == core)
@@ -206,8 +217,8 @@
 
 
 def weave(main, side, each):
-    for k, _ in enumerate(main):
-        if k % each == each - 1:
+    for _ in main:
+        for _ in range(each):
             next(side, None)
 
 
@@ -306,15 +317,15 @@
     wb[shard, pl.ds(0, units)] = wg[...]
     wb[shard, pl.ds(units, units)] = wu[...]
     wb[shard, pl.ds(2 * units, units)] = wd[...]
-    pl.semaphore_wait(barrier, 7)
-
-    weights = gather_weights(nets[0], at, wa, part)
+    pl.semaphore_wait(barrier, 10)
+
+    weights = gather_weights(nets[0], at, wa, part, True)
     next(weights)
-    weave(gather_rows(nets[2], at, normed, rows, chunks), weights, 1)
+    weave(gather_rows(nets[2], at, normed, rows, chunks), weights, 2)
     finish(weights)
-
-    weights = gather_weights(nets[1], at, wb, part)
+    weights = gather_weights(nets[1], at, wb, part, False)
     next(weights)
+
 
     def project(k, carry):
         columns = pl.ds(pl.multiple_of(k * step, step), step)
@@ -322,12 +333,8 @@
         return carry
 
     lax.fori_loop(0, qkv.shape[1] // step, project, 0)
-    for _ in range(4):
-        next(weights)
     attended = attention(qkv, seg, slot, freq, ck, cv)
     spread[...] = nn(attended, spare_columns()).astype(BF16)
-    for _ in range(4):
-        next(weights)
 
     def expand(start, size):
         def tile(k, carry):
@@ -340,7 +347,7 @@
     def add_attention(columns, total):
         middle[:, columns] = (tokens[:, columns].astype(F32) + total).astype(BF16)
 
-    weave(sum_rows(nets[3], at, terms, held, rows, chunks, expand, add_attention), weights, 2)
+    weave(sum_rows(nets[3], at, terms, held, rows, chunks, expand, add_attention), weights, 1)
     normed2[mine, :] = norm_rows(middle[...].astype(F32), gain2[...])
     weave(gather_rows(nets[4], at, normed2, rows, chunks), weights, 1)
     finish(weights)

time: 120 us -> 109 us (0.908)
  Pallas kernels: 115 us -> 104 us
    pallas_call x1, Pallas kernels: 115 us -> 104 us  [per_device(): pl.pallas_call(layer, name='layer', out_shape=(jax.ShapeDtypeStruct((rows...]
where the time goes in v3:
time: 109 us; the launch traced here: 108 us
  Pallas kernels  104 us (95%)
  local copies, waits for them, and re-layouts  3.22 us (3%)
    pallas_call x1, Pallas kernels, per_device(): pl.pallas_call(layer, name='layer', out_shape=(jax.ShapeDtypeStruct((rows...  104 us
    unnamed x7, local copies, waits for them, and re-layouts  3.22 us

profile of v3, /device:TPU:6, one launch (start us, length us, event | category | flops | bytes accessed | tf_op | source)
XLA Modules:
  0.0 108.2 jit_solution(15605437643248162061)
XLA Ops:
  0.6 104.4 %layer.1 = (bf16[32,3072]{1,0:T(8,128)(2,1)}, bf16[192,256]{1,0:T(8,128)(2,1)}, bf16[192,256]{1,0:T(8,128)(2,1)}) custom-call(bf16[32,3072]{1,0:T(8,128)(2,1)} %tokens.1, f32[1,3072]{1,0:T(1,128)} %bitcast.10, bf16[48,192]{1,0:T(8,128)(2,1)} %wq.1, bf16[48,192]{1,0:T(8,128)(2,1)} %wk.1, bf16[48,192]{1,0:T(8,128)(2,1)} %wv.1, bf16[48,192]{1,0:T(8,128)(2,1)} %bitcast.9, ...), custom_call_target="tpu_custom_call" | custom-call | tf_op jit(solution)/shard_map/layer/pallas_call | solution.py:392
  105.0 0.0 copy-start.1
  105.0 1.6 %copy.19 = bf16[32,3072]{1,0:T(8,128)(2,1)} copy(bf16[32,3072]{1,0:T(8,128)(2,1)} %get-tuple-element.12) | data formatting | bytes 393216
  106.7 0.0 copy-done.1
  106.7 0.0 copy-start
  106.7 0.6 copy.20
  107.3 0.3 copy-done
  107.6 0.6 copy.21
Async XLA Ops:
  105.0 1.7 %copy-start.1 = (bf16[192,256]{1,0:T(8,128)(2,1)S(1)}, bf16[192,256]{1,0:T(8,128)(2,1)}, u32[]{:S(2)}) copy-start(bf16[192,256]{1,0:T(8,128)(2,1)} %get-tuple-element.7) | copy-start | bytes 294916
  106.7 0.9 copy-start

commit v4 on v3

--- a/solution.py
+++ b/solution.py
@@ -156,27 +156,41 @@
     return (4, 3) if chunk % 2 == 0 else (3, 4)
 
 
-def gather_rows(net, at, whole, rows, chunks):
+def gather_rows(net, at, whole, rows, chunks, prepare=None, arrived=None):
     width = whole.shape[1] // chunks
 
     def block(dy, chunk):
         start = pl.multiple_of(wrap(at.y, dy, NY) * rows, rows)
         return whole.at[pl.ds(start, rows), pl.ds(chunk * width, width)]
 
-    flight = {}
+    flight, last = {}, []
     for step in range(1, 5):
         for chunk in range(chunks):
+            if step == 1 and prepare is not None:
+                prepare()
             for way in (0, 1):
                 sign = 1 if way == 0 else -1
                 if step > ways(chunk)[way]:
                     continue
                 if step > 1:
-                    flight[chunk, way].wait_recv()
+                    flight.pop((chunk, way)).wait_recv()
                 ref = block(-sign * (step - 1), chunk)
                 flight[chunk, way] = net.put(ref, ref, at.device(dy=sign))
+                if step == 4:
+                    last.append(flight.pop((chunk, way)))
             yield
+        if arrived is not None and step < 4:
+            for dy in ((0,) if step == 1 else (step - 1, 1 - step)):
+                arrived(dy)
     for copy in flight.values():
         copy.wait_recv()
+    if arrived is not None:
+        arrived(3)
+        arrived(-3)
+    for copy in last:
+        copy.wait_recv()
+    if arrived is not None:
+        arrived(4)
     net.sent(whole.at[pl.ds(0, (NY - 1) * rows), :], at.device(dy=1))
 
 
@@ -298,7 +312,7 @@
 def layer(
     tokens, gain, wq, wk, wv, wo, gain2, wg, wu, wd, seg, slot, freq,
     out, ck, cv,
-    wa, wb, normed, normed2, qkv, spread, terms, terms2, hidden, held, held2, middle, send, recv_w, recv_y,
+    wa, wb, normed, normed2, qkv, spread, terms, terms2, hidden, held, held2, middles, done, keys, values, send, recv_w, recv_y, local,
 ):
     at = Place()
     rows, width = tokens.shape
@@ -306,23 +320,31 @@
     step, chunks = 256, 4
     nets = [Net(send.at[k], recv_w.at[k]) for k in range(2)] + [Net(send.at[2 + k], recv_y.at[k]) for k in range(4)]
 
+    copies = []
+    taken = iter(range(9))
+
+    def keep(src, dst):
+        copy = pltpu.make_async_copy(src, dst, local.at[next(taken)])
+        copy.start()
+        return copy
+
     barrier = pltpu.get_barrier_semaphore()
     for device in at.neighbours():
         pl.semaphore_signal(barrier, inc=1, device_id=device, device_id_type=MESH)
 
     mine = pl.ds(pl.multiple_of(at.y * rows, rows), rows)
     shard = pl.ds(pl.multiple_of(at.index(0, 0, at.core) * part, part), part)
+    packed = [keep(ref, wb.at[shard, pl.ds(k * units, units)]) for k, ref in enumerate((wg, wu, wd))]
     normed[mine, :] = norm_rows(tokens[...].astype(F32), gain[...])
     pack_attention(wq, wk, wv, wo, wa.at[shard, :])
-    wb[shard, pl.ds(0, units)] = wg[...]
-    wb[shard, pl.ds(units, units)] = wu[...]
-    wb[shard, pl.ds(2 * units, units)] = wd[...]
     pl.semaphore_wait(barrier, 10)
 
     weights = gather_weights(nets[0], at, wa, part, True)
     next(weights)
     weave(gather_rows(nets[2], at, normed, rows, chunks), weights, 2)
     finish(weights)
+    for copy in packed:
+        copy.wait()
     weights = gather_weights(nets[1], at, wb, part, False)
     next(weights)
 
@@ -333,7 +355,8 @@
         return carry
 
     lax.fori_loop(0, qkv.shape[1] // step, project, 0)
-    attended = attention(qkv, seg, slot, freq, ck, cv)
+    attended = attention(qkv, seg, slot, freq, keys, values)
+    copies += [keep(keys, ck), keep(values, cv)]
     spread[...] = nn(attended, spare_columns()).astype(BF16)
 
     def expand(start, size):
@@ -345,11 +368,19 @@
         lax.fori_loop(0, size // step, tile, 0)
 
     def add_attention(columns, total):
-        middle[:, columns] = (tokens[:, columns].astype(F32) + total).astype(BF16)
-
-    weave(sum_rows(nets[3], at, terms, held, rows, chunks, expand, add_attention), weights, 1)
-    normed2[mine, :] = norm_rows(middle[...].astype(F32), gain2[...])
-    weave(gather_rows(nets[4], at, normed2, rows, chunks), weights, 1)
+        middles[mine, columns] = (tokens[:, columns].astype(F32) + total).astype(BF16)
+
+    summed = sum_rows(nets[3], at, terms, held, rows, chunks, expand, add_attention)
+    for _ in range(4 * chunks):
+        next(summed)
+        next(weights, None)
+
+    def normalise(dy):
+        block = pl.ds(pl.multiple_of(wrap(at.y, dy, NY) * rows, rows), rows)
+        normed2[block, :] = norm_rows(middles[block, :].astype(F32), gain2[...])
+
+    weave(gather_rows(nets[4], at, middles, rows, chunks, lambda: next(summed), normalise), weights, 1)
+    finish(summed)
     finish(weights)
 
     def gated(k, carry):
@@ -371,9 +402,12 @@
         lax.fori_loop(0, size // step, tile, 0)
 
     def add_mlp(columns, total):
-        out[:, columns] = (middle[:, columns].astype(F32) + total).astype(BF16)
+        done[:, columns] = (middles[mine, columns].astype(F32) + total).astype(BF16)
+        copies.append(keep(done.at[:, columns], out.at[:, columns]))
 
     finish(sum_rows(nets[5], at, terms2, held2, rows, chunks, lower, add_mlp))
+    for copy in copies:
+        copy.wait()
 
 
 def frequencies():
@@ -388,7 +422,7 @@
     heads = w_query.shape[1]
     units = w_gate.shape[1]
     count = rows * NY
-    vmem = pl.BlockSpec(memory_space=pltpu.VMEM)
+    vmem, hbm = pl.BlockSpec(memory_space=pltpu.VMEM), pl.BlockSpec(memory_space=pl.ANY)
     layer_out, keys, values = pl.pallas_call(
         layer,
         name="layer",
@@ -397,8 +431,8 @@
             jax.ShapeDtypeStruct((heads, count), BF16),
             jax.ShapeDtypeStruct((heads, count), BF16),
         ),
-        in_specs=[vmem] * 13,
-        out_specs=(vmem,) * 3,
+        in_specs=[vmem] * 7 + [hbm] * 3 + [vmem] * 3,
+        out_specs=(hbm,) * 3,
         scratch_shapes=[
             pltpu.VMEM((width, 6 * LANES), BF16),
             pltpu.VMEM((width, 3 * units), BF16),
@@ -411,10 +445,14 @@
             pltpu.VMEM((count, units), BF16),
             pltpu.VMEM((2, 4, rows, width), BF16),
             pltpu.VMEM((2, 4, rows, width), BF16),
+            pltpu.VMEM((count, width), BF16),
             pltpu.VMEM((rows, width), BF16),
+            pltpu.VMEM((heads, count), BF16),
+            pltpu.VMEM((heads, count), BF16),
             pltpu.SemaphoreType.DMA((6,)),
             pltpu.SemaphoreType.DMA((2, NX * NZ + 1)),
             pltpu.SemaphoreType.DMA((4, 28)),
+            pltpu.SemaphoreType.DMA((9,)),
         ],
         compiler_params=pltpu.CompilerParams(
             collective_id=0, has_side_effects=True, vmem_limit_bytes=56 * 2**20

time: 109 us -> 107 us (0.982)
  Pallas kernels: 104 us -> 102 us
    pallas_call x1, Pallas kernels: 104 us -> 102 us  [per_device(): pl.pallas_call(layer, name='layer', out_shape=(jax.ShapeDtypeStruct((rows...]
where the time goes in v4:
time: 107 us; the launch traced here: 106 us
  Pallas kernels  102 us (95%)
  local copies, waits for them, and re-layouts  3.22 us (3%)
    pallas_call x1, Pallas kernels, per_device(): pl.pallas_call(layer, name='layer', out_shape=(jax.ShapeDtypeStruct((rows...  102 us
    unnamed x7, local copies, waits for them, and re-layouts  3.22 us

profile of v4, /device:TPU:6, one launch (start us, length us, event | category | flops | bytes accessed | tf_op | source)
XLA Modules:
  0.0 105.8 jit_solution(7054860971332249942)
XLA Ops:
  0.6 101.9 %layer.1 = (bf16[32,3072]{1,0:T(8,128)(2,1)}, bf16[192,256]{1,0:T(8,128)(2,1)}, bf16[192,256]{1,0:T(8,128)(2,1)}) custom-call(bf16[32,3072]{1,0:T(8,128)(2,1)} %tokens.1, f32[1,3072]{1,0:T(1,128)} %bitcast.10, bf16[48,192]{1,0:T(8,128)(2,1)} %wq.1, bf16[48,192]{1,0:T(8,128)(2,1)} %wk.1, bf16[48,192]{1,0:T(8,128)(2,1)} %wv.1, bf16[48,192]{1,0:T(8,128)(2,1)} %bitcast.9, ...), custom_call_target="tpu_custom_call" | custom-call | tf_op jit(solution)/shard_map/layer/pallas_call | solution.py:426
  102.5 0.0 copy-start.1
  102.5 1.6 %copy.19 = bf16[32,3072]{1,0:T(8,128)(2,1)} copy(bf16[32,3072]{1,0:T(8,128)(2,1)} %get-tuple-element.12) | data formatting | bytes 393216
  104.2 0.0 copy-done.1
  104.2 0.0 copy-start
  104.2 0.6 copy.20
  104.8 0.3 copy-done
  105.1 0.6 copy.21
Async XLA Ops:
  102.5 1.7 %copy-start.1 = (bf16[192,256]{1,0:T(8,128)(2,1)S(1)}, bf16[192,256]{1,0:T(8,128)(2,1)}, u32[]{:S(2)}) copy-start(bf16[192,256]{1,0:T(8,128)(2,1)} %get-tuple-element.7) | copy-start | bytes 294916
  104.2 0.9 copy-start
